TPU v7x, 32 devices: a whole 2x2x4 slice. The times are simulated.
32 devices in a mesh: tile: 8 (over z, y), mem: 4 (over x, core).
Axes of the slice: x: 2, y: 2, z: 4, core: 2. Of those that a mesh axis runs over, the one named last changes fastest.
Arguments:
- control: bfloat16 [32, 16, 24576], P('mem', None, 'tile'), may hold values from -6 to 6
- ensemble: bfloat16 [32, 16, 24576], P('mem', None, 'tile'), may hold values from -1 to 1
- vertical_loc: bfloat16 [16, 16], replicated, may hold values from -1.5 to 1.5
- blocks: bfloat16 [192, 7, 128, 128], P('tile'), as said below
- edge_mask: int32 [192, 7], P('tile'), may hold values from 0 to 1, as said below
- background: float32 [16, 24576], P(None, 'tile'), may hold values from -6 to 6
- obs_precision: float32 [16, 24576], P(None, 'tile'), may hold values from 1 to 10
Outputs:
- increment: float32 [16, 24576], P('mem', 'tile')
- gradient: float32 [32, 16, 24576], P('mem', None, 'tile')
Inputs may be any that keep to these rules, and one draw needn't show every extreme that they name: `edge_mask`: each entry is 0 or 1; slot 0 is 1 for every tile; slot 2d of tile (t + d) mod 192 equals slot 2d-1 of tile t. Slot 0 blocks are symmetric, and the block in slot 2d of tile (t + d) mod 192 is the transpose of the block in slot 2d-1 of tile t, so that Lh is symmetric.
All inputs are finite; a program needn't handle non-finite values.
Results may differ from a plain program's by a relative error of at most 0.011.
Values may be sent and summed in bfloat16 or wider, within the bound.
No kernel may reach another device: no remote copies, remote signals or barrier semaphores. Data moves between devices by JAX's collectives and lax.ppermute only.
A program may use at most 64 MiB of HBM per device.

v0:
```python
import jax
import jax.numpy as jnp
from jax import lax
from jax.sharding import PartitionSpec as P


def padded_2(value, sides, width):
    for axis, dim in sides:
        size, length = (lax.axis_size(axis), value.shape[dim])
        up = [(i, (i + 1) % size) for i in range(size)]
        down = [(j, i) for i, j in up]
        last = lax.slice_in_dim(value, length - width, length, axis=dim)
        first = lax.slice_in_dim(value, 0, width, axis=dim)
        before = lax.ppermute(last, axis, up)
        after = lax.ppermute(first, axis, down)
        value = jnp.concatenate([before, value, after], axis=dim)
    return value


def passed_along(value, axis, by):
    length = lax.axis_size(axis)
    return lax.ppermute(value, axis, [(i, (i + by) % length) for i in range(length)])


def slot_offset(slot_index):
    if slot_index == 0:
        return 0
    distance = (slot_index + 1) // 2
    if slot_index % 2 == 1:
        return distance
    return -distance


def apply_rows(padded, blocks, edge_mask, tile_count):
    member_count, level_count, padded_points = padded.shape
    block_width = blocks.shape[-1]
    padded_tiles = padded.reshape(
        member_count, level_count, padded_points // block_width, block_width
    )
    reach_tiles = (padded_points // block_width - tile_count) // 2
    mask_float = edge_mask.astype(jnp.float32)
    summed = jnp.zeros((member_count, level_count, tile_count, block_width), jnp.float32)
    for slot_index in range(blocks.shape[1]):
        offset = slot_offset(slot_index)
        source = padded_tiles[:, :, reach_tiles + offset : reach_tiles + offset + tile_count]
        product = jnp.einsum(
            "tab,kltb->klta", blocks[:, slot_index], source, preferred_element_type=jnp.float32
        )
        summed = summed + mask_float[None, None, :, slot_index, None] * product
    return summed


def on_device(control, ensemble, vertical_loc, blocks, edge_mask, background, obs_precision):
    member_count, level_count, point_count = control.shape
    block_width = blocks.shape[-1]
    tile_count = point_count // block_width
    reach_tiles = (blocks.shape[1] - 1) // 2
    vertical = jnp.einsum(
        "lm,kmh->klh", vertical_loc, control, preferred_element_type=jnp.float32
    ).astype(jnp.bfloat16)
    padded = padded_2(vertical, (("tile", 2),), reach_tiles * block_width)
    localized = apply_rows(padded, blocks, edge_mask, tile_count).reshape(
        member_count, level_count, point_count
    )
    partial_sum = jnp.sum(ensemble.astype(jnp.float32) * localized, axis=0)
    row_count = level_count // lax.axis_size("mem")
    first_row = lax.axis_index("mem") * row_count
    summed_total = lax.psum(partial_sum, "mem")
    increment = lax.dynamic_slice_in_dim(summed_total, first_row, row_count, 0)
    depart = (obs_precision * (summed_total - background)).astype(jnp.bfloat16)
    weighted = (ensemble.astype(jnp.float32) * depart.astype(jnp.float32)[None]).astype(
        jnp.bfloat16
    )
    weighted_tiles = weighted.reshape(member_count, level_count, tile_count, block_width)
    mask_float = edge_mask.astype(jnp.float32)
    extended = jnp.zeros(
        (member_count, level_count, tile_count + 2 * reach_tiles, block_width), jnp.float32
    )
    for slot_index in range(blocks.shape[1]):
        offset = slot_offset(slot_index)
        contrib = jnp.einsum(
            "tab,klta->kltb",
            blocks[:, slot_index],
            weighted_tiles,
            preferred_element_type=jnp.float32,
        )
        contrib = mask_float[None, None, :, slot_index, None] * contrib
        extended = extended.at[:, :, reach_tiles + offset : reach_tiles + offset + tile_count].add(
            contrib
        )
    left_rim = extended[:, :, :reach_tiles]
    right_rim = extended[:, :, reach_tiles + tile_count :]
    from_left = passed_along(right_rim, "tile", 1)
    from_right = passed_along(left_rim, "tile", -1)
    interior = extended[:, :, reach_tiles : reach_tiles + tile_count]
    interior = interior.at[:, :, :reach_tiles].add(from_left)
    interior = interior.at[:, :, tile_count - reach_tiles :].add(from_right)
    adjoint = interior.reshape(member_count, level_count, point_count)
    gradient = control.astype(jnp.float32) + jnp.einsum(
        "ml,kmh->klh", vertical_loc.astype(jnp.float32), adjoint, precision=lax.Precision.HIGHEST
    )
    return (increment, gradient)


def solution(mesh):
    in_specs = (
        P("mem", None, "tile"),
        P("mem", None, "tile"),
        P(),
        P("tile", None, None, None),
        P("tile", None),
        P(None, "tile"),
        P(None, "tile"),
    )
    out_specs = (P("mem", "tile"), P("mem", None, "tile"))
    return jax.shard_map(
        on_device, mesh=mesh, in_specs=in_specs, out_specs=out_specs, check_vma=False
    )
```

profile of v0, /device:TPU:0, one launch (start us, length us, event | category | flops | bytes accessed | tf_op | source)
XLA Modules:
  0.0 100.6 jit_solution(4137713650633322076)
XLA Ops:
  7.9 1.5 %fusion.1 = bf16[8,16,3072]{2,1,0:T(8,128)(2,1)S(1)} fusion(bf16[8,16,3072]{2,1,0:T(8,128)(2,1)} %param.25, bf16[16,16]{1,0:T(8,128)(2,1)S(1)} %copy-done), kind=kOutput, calls=%fused_computation.3 | convolution fusion | flops 12976128 | bytes 1573376 | tf_op jit(solution)/shard_map/lm,kmh->klh/dot_general | solution.py:58
  9.4 3.0 %collective-permute-start = (bf16[8,16,384]{2,1,0:T(8,128)(2,1)S(1)}, bf16[8,16,384]{2,1,0:T(8,128)(2,1)S(1)}, u32[]{:S(2)}, u32[]{:S(2)}) collective-permute-start(bf16[8,16,384]{2,1,0:T(8,128)(2,1)S(1)} %get-tuple-element.119), channel_id=1, source_target_pairs={{0,4},{4,8},{8,12},{12,16},{16,20},{20,24},{24,28},{28,0},{1,5},{5... | collective-permute-start | bytes 294920 | tf_op jit(solution)/shard_map/ppermute | solution.py:14
  12.4 3.1 %collective-permute-start.1 = (bf16[8,16,384]{2,1,0:T(8,128)(2,1)S(1)}, bf16[8,16,384]{2,1,0:T(8,128)(2,1)S(1)}, u32[]{:S(2)}, u32[]{:S(2)}) collective-permute-start(bf16[8,16,384]{2,1,0:T(8,128)(2,1)S(1)} %get-tuple-element.120), channel_id=1, source_target_pairs={{4,0},{8,4},{12,8},{16,12},{20,16},{24,20},{28,24},{0,28},{5,1},{9... | collective-permute-start | bytes 294920 | tf_op jit(solution)/shard_map/ppermute | solution.py:15
  15.5 2.8 %collective-permute-done = bf16[8,16,384]{2,1,0:T(8,128)(2,1)S(1)} collective-permute-done((bf16[8,16,384]{2,1,0:T(8,128)(2,1)S(1)}, bf16[8,16,384]{2,1,0:T(8,128)(2,1)S(1)}, u32[]{:S(2)}, u32[]{:S(2)}) %collective-permute-start) | collective-permute-done | bytes 98336 | tf_op jit(solution)/shard_map/ppermute | solution.py:14
  19.8 1.4 %fusion.73 = (bf16[8,16,24,128]{3,2,1,0:T(8,128)(2,1)S(1)}, bf16[8,16,24,128]{3,2,1,0:T(8,128)(2,1)S(1)}, bf16[8,16,24,128]{3,2,1,0:T(8,128)(2,1)S(1)}, bf16[8,1...) fusion(bf16[8,16,30,128]{3,2,1,0:T(8,128)(2,1)S(1)} %reshape.325), kind=kLoop, calls=%fused_computation.98 | loop fusion | bytes 11010048 | tf_op jit(solution)/shard_map/slice | solution.py:45
  21.2 1.8 %fusion.22 = f32[24,8,16,128]{3,2,1,0:T(8,128)S(1)} fusion(bf16[8,16,24,128]{3,2,1,0:T(8,128)(2,1)S(1)} %get-tuple-element.113, bf16[24,7,128,128]{3,2,1,0:T(8,128)(2,1)} %param.28), kind=kOutput, calls=%fused_computation.35 | convolution fusion | flops 100663296 | bytes 3145728 | tf_op jit(solution)/shard_map/tab,kltb->klta/dot_general | solution.py:46
  23.0 1.8 %fusion.25 = f32[24,8,16,128]{3,2,1,0:T(8,128)S(1)} fusion(bf16[8,16,24,128]{3,2,1,0:T(8,128)(2,1)S(1)} %get-tuple-element.114, bf16[24,7,128,128]{3,2,1,0:T(8,128)(2,1)} %param.28), kind=kOutput, calls=%fused_computation.38 | convolution fusion | flops 100663296 | bytes 3145728 | tf_op jit(solution)/shard_map/tab,kltb->klta/dot_general | solution.py:46
  24.8 1.8 %fusion.28 = f32[24,8,16,128]{3,2,1,0:T(8,128)S(1)} fusion(bf16[8,16,24,128]{3,2,1,0:T(8,128)(2,1)S(1)} %get-tuple-element.115, bf16[24,7,128,128]{3,2,1,0:T(8,128)(2,1)} %param.28), kind=kOutput, calls=%fused_computation.41 | convolution fusion | flops 100663296 | bytes 3145728 | tf_op jit(solution)/shard_map/tab,kltb->klta/dot_general | solution.py:46
  26.6 1.8 %fusion.31 = f32[24,8,16,128]{3,2,1,0:T(8,128)S(1)} fusion(bf16[8,16,24,128]{3,2,1,0:T(8,128)(2,1)S(1)} %get-tuple-element.116, bf16[24,7,128,128]{3,2,1,0:T(8,128)(2,1)} %param.28), kind=kOutput, calls=%fused_computation.44 | convolution fusion | flops 100663296 | bytes 3145728 | tf_op jit(solution)/shard_map/tab,kltb->klta/dot_general | solution.py:46
  28.4 1.8 %fusion.34 = f32[24,8,16,128]{3,2,1,0:T(8,128)S(1)} fusion(bf16[8,16,24,128]{3,2,1,0:T(8,128)(2,1)S(1)} %get-tuple-element.117, bf16[24,7,128,128]{3,2,1,0:T(8,128)(2,1)} %param.28), kind=kOutput, calls=%fused_computation.47 | convolution fusion | flops 100663296 | bytes 3145728 | tf_op jit(solution)/shard_map/tab,kltb->klta/dot_general | solution.py:46
  30.2 1.8 %fusion.37 = f32[24,8,16,128]{3,2,1,0:T(8,128)S(1)} fusion(bf16[8,16,24,128]{3,2,1,0:T(8,128)(2,1)S(1)} %get-tuple-element.118, bf16[24,7,128,128]{3,2,1,0:T(8,128)(2,1)} %param.28), kind=kOutput, calls=%fused_computation.50 | convolution fusion | flops 100663296 | bytes 3145728 | tf_op jit(solution)/shard_map/tab,kltb->klta/dot_general | solution.py:46
  32.0 2.3 %add_bitcast_fusion = f32[24,8,2,8,128]{4,3,2,1,0:T(8,128)S(1)} fusion(f32[24,8,16,128]{3,2,1,0:T(8,128)S(1)} %fusion.22, f32[24,8,16,128]{3,2,1,0:T(8,128)S(1)} %fusion.25, f32[24,8,16,128]{3,2,1,0:T(8,128)S(1)} %fusion.28, f32[24,8,16,128]{3,2,1,0:T(8,128)S(1)} %fusion.31, f32[24,8,16,128]{3,2,1,0:T(8,128)S(1)} %fusion.34, ...), kind=kOutput, calls=%fused_computation.21 | convolution fusion | flops 105775104 | bytes 12583584 | tf_op jit(solution)/shard_map/tab,kltb->klta/dot_general | solution.py:46
  35.3 32.3 %all-reduce.3.cloned.1.call-done = f32[16,3072]{1,0:T(8,128)} async-done(((f32[16,3072]{1,0:T(8,128)}), f32[16,3072]{1,0:T(8,128)}) %all-reduce.3.cloned.1.call-update) | async-done | bytes 196624 | tf_op jit(solution)/shard_map/psum | solution.py:68
  67.6 1.0 fusion.69
  68.6 1.7 %multiply_bitcast_fusion = f32[8,16,24,128]{3,1,0,2:T(8,128)S(1)} fusion(f32[24]{0:T(128)S(1)} %get-tuple-element.121, bf16[24,7,128,128]{3,2,1,0:T(8,128)(2,1)} %param.28, bf16[8,16,3072]{2,1,0:T(8,128)(2,1)S(1)} %copy-done.1, f32[16,3072]{1,0:T(8,128)S(1)} %fusion.69), kind=kOutput, calls=%fused_computation.22 | convolution fusion | flops 102236160 | bytes 3342432 | tf_op jit(solution)/shard_map/tab,klta->kltb/dot_general | solution.py:81
  70.5 1.8 %fusion.10 = f32[8,16,30,128]{3,1,0,2:T(8,128)S(1)} fusion(f32[8,16,30,128]{3,1,0,2:T(8,128)S(1)} %scatter-add.30, f32[24]{0:T(128)S(1)} %get-tuple-element.127, bf16[24,7,128,128]{3,2,1,0:T(8,128)(2,1)} %param.28, bf16[8,16,3072]{2,1,0:T(8,128)(2,1)S(1)} %copy-done.1, f32[16,3072]{1,0:T(8,128)S(1)} %fusion.69), kind=kOutput, calls=%fused_computation.20 | convolution fusion | flops 102629376 | bytes 4915712 | tf_op jit(solution)/shard_map/tab,klta->kltb/dot_general | solution.py:81
  74.5 1.8 %constant_dynamic-update-slice_fusion = (f32[8,16,30,128]{3,1,0,2:T(8,128)S(1)}, f32[8,16,24,128]{3,1,0,2:T(8,128)}) fusion(f32[8,16,30,128]{3,1,0,2:T(8,128)S(1)} %fusion.6, bf16[24,7,128,128]{3,2,1,0:T(8,128)(2,1)S(1)} %bitcast.161, f32[24]{0:T(128)S(1)} %get-tuple-element.122, bf16[8,16,3072]{2,1,0:T(8,128)(2,1)S(1)} %copy-done.1, f32[16,3072]{1,0:T(8,128)S(1)} %fusion.69), kind=kOutput, calls=%fused_computation.88 | convolution fusion | flops 102629376 | bytes 6488576 | tf_op jit(solution)/shard_map/tab,klta->kltb/dot_general | solution.py:81
  76.3 1.5 %collective-permute-start.2 = (f32[8,16,3,128]{3,1,0,2:T(8,128)S(1)}, f32[8,16,3,128]{3,1,0,2:T(8,128)S(1)}, u32[]{:S(2)}, u32[]{:S(2)}) collective-permute-start(f32[8,16,3,128]{3,1,0,2:T(8,128)S(1)} %slice.403), channel_id=1, source_target_pairs={{0,4},{4,8},{8,12},{12,16},{16,20},{20,24},{24,28},{28,0},{1,5},{5... | collective-permute-start | bytes 589832 | tf_op jit(solution)/shard_map/ppermute | solution.py:22
  78.0 6.7 %collective-permute-done.2 = f32[8,16,3,128]{3,1,0,2:T(8,128)S(1)} collective-permute-done((f32[8,16,3,128]{3,1,0,2:T(8,128)S(1)}, f32[8,16,3,128]{3,1,0,2:T(8,128)S(1)}, u32[]{:S(2)}, u32[]{:S(2)}) %collective-permute-start.2) | collective-permute-done | bytes 196640 | tf_op jit(solution)/shard_map/ppermute | solution.py:22
  84.7 1.1 %fusion.72 = (f32[8,16,3,128]{3,1,0,2:T(8,128)S(1)}, f32[8,16,24,128]{3,1,0,2:T(8,128)S(1)}) fusion(f32[8,16,24,128]{3,1,0,2:T(8,128)} %get-tuple-element.129, f32[8,16,24,128]{3,1,0,2:T(8,128)S(1)} %slice.401, f32[8,16,3,128]{3,1,0,2:T(8,128)S(1)} %collective-permute-done.2), kind=kLoop, calls=%fused_computation.97 | loop fusion | flops 49152 | bytes 983040 | tf_op jit(solution)/shard_map/slice | solution.py:91
  85.8 1.6 %collective-permute-start.3 = (f32[8,16,3,128]{3,1,0,2:T(8,128)S(1)}, f32[8,16,3,128]{3,1,0,2:T(8,128)S(1)}, u32[]{:S(2)}, u32[]{:S(2)}) collective-permute-start(f32[8,16,3,128]{3,1,0,2:T(8,128)S(1)} %get-tuple-element.110), channel_id=1, source_target_pairs={{0,28},{4,0},{8,4},{12,8},{16,12},{20,16},{24,20},{28,24},{1,29},{... | collective-permute-start | bytes 589832 | tf_op jit(solution)/shard_map/ppermute | solution.py:22
  87.4 1.5 %constant_dynamic-slice_fusion = f32[4,3072]{1,0:T(4,128)} fusion(f32[16,3072]{1,0:T(8,128)} %all-reduce.3.cloned.1.call-done, s32[]{:T(128)S(6)} %select_n.3), kind=kLoop, calls=%fused_computation.89 | loop fusion | bytes 98308 | tf_op jit(solution)/shard_map/dynamic_slice | solution.py:69
  88.9 2.6 %collective-permute-done.3 = f32[8,16,3,128]{3,1,0,2:T(8,128)S(1)} collective-permute-done((f32[8,16,3,128]{3,1,0,2:T(8,128)S(1)}, f32[8,16,3,128]{3,1,0,2:T(8,128)S(1)}, u32[]{:S(2)}, u32[]{:S(2)}) %collective-permute-start.3) | collective-permute-done | bytes 196640 | tf_op jit(solution)/shard_map/ppermute | solution.py:22
  91.6 2.1 %fusion = f32[8,16,3072]{2,1,0:T(8,128)} fusion(bf16[8,16,3072]{2,1,0:T(8,128)(2,1)S(1)} %copy-done.2, bf16[16,16]{1,0:T(8,128)(2,1)S(1)} %copy-done, f32[8,16,24,128]{3,1,0,2:T(8,128)S(1)} %fusion.67), kind=kOutput, calls=%fused_computation.1 | convolution fusion | flops 76283904 | bytes 3932672 | tf_op jit(solution)/shard_map/ml,kmh->klh/dot_general | solution.py:99
  (34 shorter events, 5.7 us)
Async XLA Ops:
  7.2 0.7 copy-start
  7.2 8.3 %copy-start.5 = (s32[24,7]{0,1:T(8,128)S(1)}, s32[24,7]{0,1:T(8,128)}, u32[]{:S(2)}) copy-start(s32[24,7]{0,1:T(8,128)} %param.29) | copy-start | bytes 2020
  7.2 60.4 %all-reduce.3.cloned.1.call-start = ((), (), s32[]{:S(2)}) async-start(), calls=%async_computation | async-start | bytes 393216 | tf_op jit(solution)/shard_map/psum | solution.py:68
  9.4 9.0 %collective-permute-start = (bf16[8,16,384]{2,1,0:T(8,128)(2,1)S(1)}, bf16[8,16,384]{2,1,0:T(8,128)(2,1)S(1)}, u32[]{:S(2)}, u32[]{:S(2)}) collective-permute-start(bf16[8,16,384]{2,1,0:T(8,128)(2,1)S(1)} %get-tuple-element.119), channel_id=1, source_target_pairs={{0,4},{4,8},{8,12},{12,16},{16,20},{20,24},{24,28},{28,0},{1,5},{5... | collective-permute-start | bytes 294920 | tf_op jit(solution)/shard_map/ppermute | solution.py:14
  12.4 6.7 %collective-permute-start.1 = (bf16[8,16,384]{2,1,0:T(8,128)(2,1)S(1)}, bf16[8,16,384]{2,1,0:T(8,128)(2,1)S(1)}, u32[]{:S(2)}, u32[]{:S(2)}) collective-permute-start(bf16[8,16,384]{2,1,0:T(8,128)(2,1)S(1)} %get-tuple-element.120), channel_id=1, source_target_pairs={{4,0},{8,4},{12,8},{16,12},{20,16},{24,20},{28,24},{0,28},{5,1},{9... | collective-permute-start | bytes 294920 | tf_op jit(solution)/shard_map/ppermute | solution.py:15
  32.0 2.3 %copy-start.1 = (bf16[8,16,3072]{2,1,0:T(8,128)(2,1)S(1)}, bf16[8,16,3072]{2,1,0:T(8,128)(2,1)}, u32[]{:S(2)}) copy-start(bf16[8,16,3072]{2,1,0:T(8,128)(2,1)} %param.26) | copy-start | bytes 2359300
  34.3 33.2 %copy-start.3 = (f32[16,3072]{1,0:T(8,128)S(1)}, f32[16,3072]{1,0:T(8,128)}, u32[]{:S(2)}) copy-start(f32[16,3072]{1,0:T(8,128)} %param.31) | copy-start | bytes 589828
  34.4 33.2 %copy-start.4 = (f32[16,3072]{1,0:T(8,128)S(1)}, f32[16,3072]{1,0:T(8,128)}, u32[]{:S(2)}) copy-start(f32[16,3072]{1,0:T(8,128)} %param.30) | copy-start | bytes 589828
  68.6 3.7 %slice-start = ((s8[5505024]{0:T(1024)(128)(4,1)}), s8[4194304]{0:T(1024)(128)(4,1)S(1)}, s32[]{:S(2)}) async-start(s8[5505024]{0:T(1024)(128)(4,1)} %bitcast.160), calls=%async_computation.1 | async-start | bytes 8388608
  70.3 2.0 %slice-start.1 = ((s8[5505024]{0:T(1024)(128)(4,1)}), s8[1310720]{0:T(1024)(128)(4,1)S(1)}, s32[]{:S(2)}) async-start(s8[5505024]{0:T(1024)(128)(4,1)} %bitcast.160), calls=%async_computation.2 | async-start | bytes 2621440
  76.3 8.4 %collective-permute-start.2 = (f32[8,16,3,128]{3,1,0,2:T(8,128)S(1)}, f32[8,16,3,128]{3,1,0,2:T(8,128)S(1)}, u32[]{:S(2)}, u32[]{:S(2)}) collective-permute-start(f32[8,16,3,128]{3,1,0,2:T(8,128)S(1)} %slice.403), channel_id=1, source_target_pairs={{0,4},{4,8},{8,12},{12,16},{16,20},{20,24},{24,28},{28,0},{1,5},{5... | collective-permute-start | bytes 589832 | tf_op jit(solution)/shard_map/ppermute | solution.py:22
  78.0 13.6 %copy-start.2 = (bf16[8,16,3072]{2,1,0:T(8,128)(2,1)S(1)}, bf16[8,16,3072]{2,1,0:T(8,128)(2,1)}, u32[]{:S(2)}) copy-start(bf16[8,16,3072]{2,1,0:T(8,128)(2,1)} %param.25) | copy-start | bytes 2359300
  85.8 5.7 %collective-permute-start.3 = (f32[8,16,3,128]{3,1,0,2:T(8,128)S(1)}, f32[8,16,3,128]{3,1,0,2:T(8,128)S(1)}, u32[]{:S(2)}, u32[]{:S(2)}) collective-permute-start(f32[8,16,3,128]{3,1,0,2:T(8,128)S(1)} %get-tuple-element.110), channel_id=1, source_target_pairs={{0,28},{4,0},{8,4},{12,8},{16,12},{20,16},{24,20},{28,24},{1,29},{... | collective-permute-start | bytes 589832 | tf_op jit(solution)/shard_map/ppermute | solution.py:22
Sparse Core Ops, SparseCore 0:
  35.4 32.1 all-reduce.2
where the time goes:
time: 101 us
  waiting for transfers between devices  45.3 us (45%)
  matrix products  24.1 us (24%)
  between operations  14.3 us (14%)
  starting transfers between devices  9.29 us (9%)
  local copies, waits for them, and re-layouts  4.6 us (5%)
  other arithmetic  3.06 us (3%)
    psum x1, waiting for transfers between devices, on_device(): summed_total = lax.psum(partial_sum, 'mem')  32.3 us
    dot_general x7, matrix products, apply_rows(): jnp.einsum('tab,kltb->klta', blocks[:, slot_index], source, preferred_ele...  13.1 us
    ppermute x2, waiting for transfers between devices, passed_along(): lax.ppermute(value, axis, [(i, (i + by) % length) for i in range(length)])  9.32 us
    dot_general x7, matrix products, on_device(): jnp.einsum('tab,klta->kltb', blocks[:, slot_index], weighted_tiles, prefe...  7.37 us
    ppermute x2, starting transfers between devices, passed_along(): lax.ppermute(value, axis, [(i, (i + by) % length) for i in range(length)])  3.13 us
    ppermute x1, starting transfers between devices, padded_2(): after = lax.ppermute(first, axis, down)  3.1 us
    ppermute x1, starting transfers between devices, padded_2(): before = lax.ppermute(last, axis, up)  3.02 us
    ppermute x1, waiting for transfers between devices, padded_2(): before = lax.ppermute(last, axis, up)  2.82 us
  transfers between devices with their start and end apart: 5, of which 5 were waited for; matrix products, arithmetic and copies ran while one was open for 2% of the time, Pallas kernels for 0%

commit v1 on v0

--- a/solution.py
+++ b/solution.py
@@ -65,7 +65,11 @@
     partial_sum = jnp.sum(ensemble.astype(jnp.float32) * localized, axis=0)
     row_count = level_count // lax.axis_size("mem")
     first_row = lax.axis_index("mem") * row_count
-    summed_total = lax.psum(partial_sum, "mem")
+    summed_total = partial_sum
+    for hop in (1, 2):
+        summed_total = summed_total + lax.ppermute(
+            summed_total, "mem", [(dev, dev ^ hop) for dev in range(4)]
+        )
     increment = lax.dynamic_slice_in_dim(summed_total, first_row, row_count, 0)
     depart = (obs_precision * (summed_total - background)).astype(jnp.bfloat16)
     weighted = (ensemble.astype(jnp.float32) * depart.astype(jnp.float32)[None]).astype(

time: 101 us -> 57.3 us (0.57)
  waiting for transfers between devices: 45.3 us -> 22.3 us
  between operations: 14.3 us -> 0.9 us
  matrix products: 24.1 us -> 17.4 us
  other arithmetic: 3.06 us -> 2.05 us
    psum x1 -> x0, waiting for transfers between devices: 32.3 us -> none  [on_device(): summed_total = lax.psum(partial_sum, 'mem')]
    ppermute x0 -> x2, waiting for transfers between devices: none -> 6.88 us  [on_device(): lax.ppermute(summed_total, 'mem', [(dev, dev ^ hop) for dev in range(4)])]
    dot_general x7, matrix products: 7.37 us -> 3.73 us  [on_device(): jnp.einsum('tab,klta->kltb', blocks[:, slot_index], weighted_tiles, prefe...]
    dot_general x7, matrix products: 13.1 us -> 10 us  [apply_rows(): jnp.einsum('tab,kltb->klta', blocks[:, slot_index], source, preferred_ele...]
    ppermute x2, waiting for transfers between devices: 9.32 us -> 11.8 us  [passed_along(): lax.ppermute(value, axis, [(i, (i + by) % length) for i in range(length)])]
    ppermute x2, starting transfers between devices: 3.13 us -> 1.36 us  [passed_along(): lax.ppermute(value, axis, [(i, (i + by) % length) for i in range(length)])]
    ppermute x0 -> x2, starting transfers between devices: none -> 1.63 us  [on_device(): lax.ppermute(summed_total, 'mem', [(dev, dev ^ hop) for dev in range(4)])]
  transfers between devices with their start and end apart: 5 -> 6, of which waited for: 5 -> 6; matrix products, arithmetic and copies ran while one was open for 2% -> 3% of each run, Pallas kernels for 0% -> 0%
where the time goes in v1:
time: 57.3 us; the launch traced here: 57 us
  waiting for transfers between devices  22.3 us (39%)
  matrix products  17.4 us (30%)
  starting transfers between devices  9.1 us (16%)
  local copies, waits for them, and re-layouts  5.31 us (9%)
  other arithmetic  2.05 us (4%)
  between operations  0.9 us (2%)
    ppermute x2, waiting for transfers between devices, passed_along(): lax.ppermute(value, axis, [(i, (i + by) % length) for i in range(length)])  11.8 us
    dot_general x7, matrix products, apply_rows(): jnp.einsum('tab,kltb->klta', blocks[:, slot_index], source, preferred_ele...  10 us
    ppermute x2, waiting for transfers between devices, on_device(): lax.ppermute(summed_total, 'mem', [(dev, dev ^ hop) for dev in range(4)])  6.88 us
    dot_general x7, matrix products, on_device(): jnp.einsum('tab,klta->kltb', blocks[:, slot_index], weighted_tiles, prefe...  3.73 us
    ppermute x1, starting transfers between devices, padded_2(): after = lax.ppermute(first, axis, down)  3.1 us
    ppermute x1, starting transfers between devices, padded_2(): before = lax.ppermute(last, axis, up)  3.02 us
    ppermute x1, waiting for transfers between devices, padded_2(): before = lax.ppermute(last, axis, up)  2.82 us
    dot_general x1, matrix products, on_device(): jnp.einsum('ml,kmh->klh', vertical_loc.astype(jnp.float32), adjoint, prec...  2.15 us
  transfers between devices with their start and end apart: 6, of which 6 were waited for; matrix products, arithmetic and copies ran while one was open for 3% of the time, Pallas kernels for 0%

profile of v1, /device:TPU:0, one launch (start us, length us, event | category | flops | bytes accessed | tf_op | source)
XLA Modules:
  0.0 57.0 jit_solution(7576305399718632632)
XLA Ops:
  0.7 0.7 %copy-done = bf16[16,16]{1,0:T(8,128)(2,1)S(1)} copy-done((bf16[16,16]{1,0:T(8,128)(2,1)S(1)}, bf16[16,16]{1,0:T(8,128)(2,1)}, u32[]{:S(2)}) %copy-start) | copy-done | bytes 536
  1.3 1.5 %fusion.1 = bf16[8,16,3072]{2,1,0:T(8,128)(2,1)S(1)} fusion(bf16[8,16,3072]{2,1,0:T(8,128)(2,1)} %param.25, bf16[16,16]{1,0:T(8,128)(2,1)S(1)} %copy-done), kind=kOutput, calls=%fused_computation.3 | convolution fusion | flops 12976128 | bytes 1573376 | tf_op jit(solution)/shard_map/lm,kmh->klh/dot_general | solution.py:58
  2.8 3.0 %collective-permute-start = (bf16[8,16,384]{2,1,0:T(8,128)(2,1)S(1)}, bf16[8,16,384]{2,1,0:T(8,128)(2,1)S(1)}, u32[]{:S(2)}, u32[]{:S(2)}) collective-permute-start(bf16[8,16,384]{2,1,0:T(8,128)(2,1)S(1)} %get-tuple-element.121), channel_id=1, source_target_pairs={{0,4},{4,8},{8,12},{12,16},{16,20},{20,24},{24,28},{28,0},{1,5},{5... | collective-permute-start | bytes 294920 | tf_op jit(solution)/shard_map/ppermute | solution.py:14
  5.8 3.1 %collective-permute-start.1 = (bf16[8,16,384]{2,1,0:T(8,128)(2,1)S(1)}, bf16[8,16,384]{2,1,0:T(8,128)(2,1)S(1)}, u32[]{:S(2)}, u32[]{:S(2)}) collective-permute-start(bf16[8,16,384]{2,1,0:T(8,128)(2,1)S(1)} %get-tuple-element.122), channel_id=1, source_target_pairs={{4,0},{8,4},{12,8},{16,12},{20,16},{24,20},{28,24},{0,28},{5,1},{9... | collective-permute-start | bytes 294920 | tf_op jit(solution)/shard_map/ppermute | solution.py:15
  9.0 2.8 %collective-permute-done = bf16[8,16,384]{2,1,0:T(8,128)(2,1)S(1)} collective-permute-done((bf16[8,16,384]{2,1,0:T(8,128)(2,1)S(1)}, bf16[8,16,384]{2,1,0:T(8,128)(2,1)S(1)}, u32[]{:S(2)}, u32[]{:S(2)}) %collective-permute-start) | collective-permute-done | bytes 98336 | tf_op jit(solution)/shard_map/ppermute | solution.py:14
  11.8 0.8 %collective-permute-done.1 = bf16[8,16,384]{2,1,0:T(8,128)(2,1)S(1)} collective-permute-done((bf16[8,16,384]{2,1,0:T(8,128)(2,1)S(1)}, bf16[8,16,384]{2,1,0:T(8,128)(2,1)S(1)}, u32[]{:S(2)}, u32[]{:S(2)}) %collective-permute-start.1) | collective-permute-done | bytes 98336 | tf_op jit(solution)/shard_map/ppermute | solution.py:15
  13.3 1.4 %fusion.73 = (bf16[8,16,24,128]{3,2,1,0:T(8,128)(2,1)S(1)}, bf16[8,16,24,128]{3,2,1,0:T(8,128)(2,1)S(1)}, bf16[8,16,24,128]{3,2,1,0:T(8,128)(2,1)S(1)}, bf16[8,1...) fusion(bf16[8,16,30,128]{3,2,1,0:T(8,128)(2,1)S(1)} %reshape.325), kind=kLoop, calls=%fused_computation.98 | loop fusion | bytes 11010048 | tf_op jit(solution)/shard_map/slice | solution.py:45
  14.7 1.9 %fusion.22 = f32[24,8,16,128]{3,2,1,0:T(8,128)S(1)} fusion(bf16[8,16,24,128]{3,2,1,0:T(8,128)(2,1)S(1)} %get-tuple-element.115, bf16[24,7,128,128]{3,2,1,0:T(8,128)(2,1)} %param.28), kind=kOutput, calls=%fused_computation.35 | convolution fusion | flops 100663296 | bytes 3145728 | tf_op jit(solution)/shard_map/tab,kltb->klta/dot_general | solution.py:46
  16.7 1.8 %fusion.25 = f32[24,8,16,128]{3,2,1,0:T(8,128)S(1)} fusion(bf16[8,16,24,128]{3,2,1,0:T(8,128)(2,1)S(1)} %get-tuple-element.116, bf16[24,7,128,128]{3,2,1,0:T(8,128)(2,1)} %param.28), kind=kOutput, calls=%fused_computation.38 | convolution fusion | flops 100663296 | bytes 3145728 | tf_op jit(solution)/shard_map/tab,kltb->klta/dot_general | solution.py:46
  18.5 1.8 %fusion.28 = f32[24,8,16,128]{3,2,1,0:T(8,128)S(1)} fusion(bf16[8,16,24,128]{3,2,1,0:T(8,128)(2,1)S(1)} %get-tuple-element.117, bf16[24,7,128,128]{3,2,1,0:T(8,128)(2,1)} %param.28), kind=kOutput, calls=%fused_computation.41 | convolution fusion | flops 100663296 | bytes 3145728 | tf_op jit(solution)/shard_map/tab,kltb->klta/dot_general | solution.py:46
  20.3 1.8 %fusion.31 = f32[24,8,16,128]{3,2,1,0:T(8,128)S(1)} fusion(bf16[8,16,24,128]{3,2,1,0:T(8,128)(2,1)S(1)} %get-tuple-element.118, bf16[24,7,128,128]{3,2,1,0:T(8,128)(2,1)} %param.28), kind=kOutput, calls=%fused_computation.44 | convolution fusion | flops 100663296 | bytes 3145728 | tf_op jit(solution)/shard_map/tab,kltb->klta/dot_general | solution.py:46
  22.8 0.7 %fusion.37 = f32[24,8,16,128]{3,2,1,0:T(8,128)S(1)} fusion(bf16[8,16,24,128]{3,2,1,0:T(8,128)(2,1)S(1)} %get-tuple-element.120, bf16[24,7,128,128]{3,2,1,0:T(8,128)(2,1)S(1)} %bitcast.161), kind=kOutput, calls=%fused_computation.50 | convolution fusion | flops 100663296 | bytes 3145728 | tf_op jit(solution)/shard_map/tab,kltb->klta/dot_general | solution.py:46
  23.4 1.4 %add_bitcast_fusion = f32[24,8,2,8,128]{4,3,2,1,0:T(8,128)S(1)} fusion(f32[24,8,16,128]{3,2,1,0:T(8,128)S(1)} %fusion.22, f32[24,8,16,128]{3,2,1,0:T(8,128)S(1)} %fusion.25, f32[24,8,16,128]{3,2,1,0:T(8,128)S(1)} %fusion.28, f32[24,8,16,128]{3,2,1,0:T(8,128)S(1)} %fusion.31, f32[24,8,16,128]{3,2,1,0:T(8,128)S(1)} %fusion.34, ...), kind=kOutput, calls=%fused_computation.21 | convolution fusion | flops 105775104 | bytes 12586496 | tf_op jit(solution)/shard_map/tab,kltb->klta/dot_general | solution.py:46
  25.1 1.4 %collective-permute-done.2 = f32[16,3072]{1,0:T(8,128)S(1)} collective-permute-done((f32[16,3072]{1,0:T(8,128)S(1)}, f32[16,3072]{1,0:T(8,128)S(1)}, u32[]{:S(2)}, u32[]{:S(2)}) %collective-permute-start.2) | collective-permute-done | bytes 196640 | tf_op jit(solution)/shard_map/ppermute | solution.py:70
  26.6 1.6 %collective-permute-start.3 = (f32[16,3072]{1,0:T(8,128)S(1)}, f32[16,3072]{1,0:T(8,128)S(1)}, u32[]{:S(2)}, u32[]{:S(2)}) collective-permute-start(f32[16,3072]{1,0:T(8,128)S(1)} %add.105), channel_id=1, source_target_pairs={{0,2},{1,3},{2,0},{3,1},{4,6},{5,7},{6,4},{7,5},{8,10},{9,11},{10,... | collective-permute-start | bytes 589832 | tf_op jit(solution)/shard_map/ppermute | solution.py:70
  28.1 5.5 %collective-permute-done.3 = f32[16,3072]{1,0:T(8,128)S(1)} collective-permute-done((f32[16,3072]{1,0:T(8,128)S(1)}, f32[16,3072]{1,0:T(8,128)S(1)}, u32[]{:S(2)}, u32[]{:S(2)}) %collective-permute-start.3) | collective-permute-done | bytes 196640 | tf_op jit(solution)/shard_map/ppermute | solution.py:70
  33.6 0.7 %fusion.69 = (f32[16,3072]{1,0:T(8,128)S(1)}, f32[16,3072]{1,0:T(8,128)}) fusion(f32[16,3072]{1,0:T(8,128)S(1)} %copy-done.3, f32[16,3072]{1,0:T(8,128)S(1)} %copy-done.4, f32[16,3072]{1,0:T(8,128)S(1)} %add.105, f32[16,3072]{1,0:T(8,128)S(1)} %collective-permute-done.3), kind=kLoop, calls=%fused_computation.85 | loop fusion | flops 245760 | bytes 1179648 | tf_op jit(solution)/shard_map/convert_element_type | solution.py:75
  38.3 0.7 %slice.403 = f32[8,16,3,128]{3,1,0,2:T(8,128)} slice(f32[8,16,30,128]{3,1,0,2:T(8,128)S(1)} %get-tuple-element.130), slice={[0:8], [0:16], [27:30], [0:128]} | slice | bytes 393216 | tf_op jit(solution)/shard_map/slice | solution.py:96
  39.5 8.6 %collective-permute-done.4 = f32[8,16,3,128]{3,1,0,2:T(8,128)} collective-permute-done((f32[8,16,3,128]{3,1,0,2:T(8,128)}, f32[8,16,3,128]{3,1,0,2:T(8,128)}, u32[]{:S(2)}, u32[]{:S(2)}) %collective-permute-start.4) | collective-permute-done | bytes 196640 | tf_op jit(solution)/shard_map/ppermute | solution.py:22
  48.1 1.0 %fusion.72 = (f32[8,16,3,128]{3,1,0,2:T(8,128)S(1)}, f32[8,16,24,128]{3,1,0,2:T(8,128)S(1)}) fusion(f32[8,16,24,128]{3,1,0,2:T(8,128)S(1)} %get-tuple-element.131, f32[8,16,24,128]{3,1,0,2:T(8,128)S(1)} %slice.401, f32[8,16,3,128]{3,1,0,2:T(8,128)} %collective-permute-done.4), kind=kLoop, calls=%fused_computation.97 | loop fusion | flops 49152 | bytes 983040 | tf_op jit(solution)/shard_map/slice | solution.py:95
  49.1 1.0 %collective-permute-start.5 = (f32[8,16,3,128]{3,1,0,2:T(8,128)S(1)}, f32[8,16,3,128]{3,1,0,2:T(8,128)S(1)}, u32[]{:S(2)}, u32[]{:S(2)}) collective-permute-start(f32[8,16,3,128]{3,1,0,2:T(8,128)S(1)} %get-tuple-element.112), channel_id=1, source_target_pairs={{0,28},{4,0},{8,4},{12,8},{16,12},{20,16},{24,20},{28,24},{1,29},{... | collective-permute-start | bytes 589832 | tf_op jit(solution)/shard_map/ppermute | solution.py:22
  50.1 1.5 %constant_dynamic-slice_fusion = f32[4,3072]{1,0:T(4,128)} fusion(f32[16,3072]{1,0:T(8,128)} %get-tuple-element.111, s32[]{:T(128)S(6)} %select_n.3), kind=kLoop, calls=%fused_computation.89 | loop fusion | bytes 98308 | tf_op jit(solution)/shard_map/dynamic_slice | solution.py:73
  51.6 3.2 %collective-permute-done.5 = f32[8,16,3,128]{3,1,0,2:T(8,128)S(1)} collective-permute-done((f32[8,16,3,128]{3,1,0,2:T(8,128)S(1)}, f32[8,16,3,128]{3,1,0,2:T(8,128)S(1)}, u32[]{:S(2)}, u32[]{:S(2)}) %collective-permute-start.5) | collective-permute-done | bytes 196640 | tf_op jit(solution)/shard_map/ppermute | solution.py:22
  54.9 2.1 %fusion = f32[8,16,3072]{2,1,0:T(8,128)} fusion(bf16[8,16,3072]{2,1,0:T(8,128)(2,1)S(1)} %copy-done.2, bf16[16,16]{1,0:T(8,128)(2,1)S(1)} %copy-done, f32[8,16,24,128]{3,1,0,2:T(8,128)S(1)} %fusion.67), kind=kOutput, calls=%fused_computation.1 | convolution fusion | flops 76283904 | bytes 3932672 | tf_op jit(solution)/shard_map/ml,kmh->klh/dot_general | solution.py:103
  (36 shorter events, 6.1 us)
Async XLA Ops:
  0.6 0.7 %copy-start = (bf16[16,16]{1,0:T(8,128)(2,1)S(1)}, bf16[16,16]{1,0:T(8,128)(2,1)}, u32[]{:S(2)}) copy-start(bf16[16,16]{1,0:T(8,128)(2,1)} %param.27) | copy-start | bytes 1540
  0.6 8.3 %copy-start.5 = (s32[24,7]{0,1:T(8,128)S(1)}, s32[24,7]{0,1:T(8,128)}, u32[]{:S(2)}) copy-start(s32[24,7]{0,1:T(8,128)} %param.29) | copy-start | bytes 2020
  2.8 9.0 %collective-permute-start = (bf16[8,16,384]{2,1,0:T(8,128)(2,1)S(1)}, bf16[8,16,384]{2,1,0:T(8,128)(2,1)S(1)}, u32[]{:S(2)}, u32[]{:S(2)}) collective-permute-start(bf16[8,16,384]{2,1,0:T(8,128)(2,1)S(1)} %get-tuple-element.121), channel_id=1, source_target_pairs={{0,4},{4,8},{8,12},{12,16},{16,20},{20,24},{24,28},{28,0},{1,5},{5... | collective-permute-start | bytes 294920 | tf_op jit(solution)/shard_map/ppermute | solution.py:14
  5.8 6.7 %collective-permute-start.1 = (bf16[8,16,384]{2,1,0:T(8,128)(2,1)S(1)}, bf16[8,16,384]{2,1,0:T(8,128)(2,1)S(1)}, u32[]{:S(2)}, u32[]{:S(2)}) collective-permute-start(bf16[8,16,384]{2,1,0:T(8,128)(2,1)S(1)} %get-tuple-element.122), channel_id=1, source_target_pairs={{4,0},{8,4},{12,8},{16,12},{20,16},{24,20},{28,24},{0,28},{5,1},{9... | collective-permute-start | bytes 294920 | tf_op jit(solution)/shard_map/ppermute | solution.py:15
  13.2 8.8 %slice-start = ((s8[5505024]{0:T(1024)(128)(4,1)}), s8[1310720]{0:T(1024)(128)(4,1)S(1)}, s32[]{:S(2)}) async-start(s8[5505024]{0:T(1024)(128)(4,1)} %bitcast.160), calls=%async_computation | async-start | bytes 2621440
  14.7 7.4 %slice-start.1 = ((s8[5505024]{0:T(1024)(128)(4,1)}), s8[4194304]{0:T(1024)(128)(4,1)S(1)}, s32[]{:S(2)}) async-start(s8[5505024]{0:T(1024)(128)(4,1)} %bitcast.160), calls=%async_computation.1 | async-start | bytes 8388608
  23.4 1.4 %copy-start.1 = (bf16[8,16,3072]{2,1,0:T(8,128)(2,1)S(1)}, bf16[8,16,3072]{2,1,0:T(8,128)(2,1)}, u32[]{:S(2)}) copy-start(bf16[8,16,3072]{2,1,0:T(8,128)(2,1)} %param.26) | copy-start | bytes 2359300
  24.8 8.8 %copy-start.3 = (f32[16,3072]{1,0:T(8,128)S(1)}, f32[16,3072]{1,0:T(8,128)}, u32[]{:S(2)}) copy-start(f32[16,3072]{1,0:T(8,128)} %param.31) | copy-start | bytes 589828
  24.8 8.8 %copy-start.4 = (f32[16,3072]{1,0:T(8,128)S(1)}, f32[16,3072]{1,0:T(8,128)}, u32[]{:S(2)}) copy-start(f32[16,3072]{1,0:T(8,128)} %param.30) | copy-start | bytes 589828
  25.0 1.5 %collective-permute-start.2 = (f32[16,3072]{1,0:T(8,128)S(1)}, f32[16,3072]{1,0:T(8,128)S(1)}, u32[]{:S(2)}, u32[]{:S(2)}) collective-permute-start(f32[16,3072]{1,0:T(8,128)S(1)} %fusion.2), channel_id=1, source_target_pairs={{0,1},{1,0},{2,3},{3,2},{4,5},{5,4},{6,7},{7,6},{8,9},{9,8},{10,11... | collective-permute-start | bytes 589832 | tf_op jit(solution)/shard_map/ppermute | solution.py:70
  26.6 7.0 %collective-permute-start.3 = (f32[16,3072]{1,0:T(8,128)S(1)}, f32[16,3072]{1,0:T(8,128)S(1)}, u32[]{:S(2)}, u32[]{:S(2)}) collective-permute-start(f32[16,3072]{1,0:T(8,128)S(1)} %add.105), channel_id=1, source_target_pairs={{0,2},{1,3},{2,0},{3,1},{4,6},{5,7},{6,4},{7,5},{8,10},{9,11},{10,... | collective-permute-start | bytes 589832 | tf_op jit(solution)/shard_map/ppermute | solution.py:70
  39.0 9.1 %collective-permute-start.4 = (f32[8,16,3,128]{3,1,0,2:T(8,128)}, f32[8,16,3,128]{3,1,0,2:T(8,128)}, u32[]{:S(2)}, u32[]{:S(2)}) collective-permute-start(f32[8,16,3,128]{3,1,0,2:T(8,128)} %slice.403), channel_id=1, source_target_pairs={{0,4},{4,8},{8,12},{12,16},{16,20},{20,24},{24,28},{28,0},{1,5},{5... | collective-permute-start | bytes 589832 | tf_op jit(solution)/shard_map/ppermute | solution.py:22
  39.5 15.4 %copy-start.2 = (bf16[8,16,3072]{2,1,0:T(8,128)(2,1)S(1)}, bf16[8,16,3072]{2,1,0:T(8,128)(2,1)}, u32[]{:S(2)}) copy-start(bf16[8,16,3072]{2,1,0:T(8,128)(2,1)} %param.25) | copy-start | bytes 2359300
  49.1 5.7 %collective-permute-start.5 = (f32[8,16,3,128]{3,1,0,2:T(8,128)S(1)}, f32[8,16,3,128]{3,1,0,2:T(8,128)S(1)}, u32[]{:S(2)}, u32[]{:S(2)}) collective-permute-start(f32[8,16,3,128]{3,1,0,2:T(8,128)S(1)} %get-tuple-element.112), channel_id=1, source_target_pairs={{0,28},{4,0},{8,4},{12,8},{16,12},{20,16},{24,20},{28,24},{1,29},{... | collective-permute-start | bytes 589832 | tf_op jit(solution)/shard_map/ppermute | solution.py:22
